TPU v7x, 128 devices: a whole 4x4x4 slice. The times are simulated.
128 devices in a mesh: row: 8 (over z_hi, y), col: 16 (over z_lo, x, core).
Axes of the slice: x: 4, y: 4, z: 4 (z_hi: 2, z_lo: 2; z = z_hi * 2 + z_lo), core: 2. Of those that a mesh axis runs over, the one named last changes fastest.
Arguments:
- node_coords: float32 [3, 131072], P(None, ('row', 'col')), may hold values from -0.08 to 66.08, as said below
- tet_nodes: int32 [4, 864000], P(None, ('row', 'col')), may hold values from -1 to 1535, as said below
- bnd_nodes: int32 [55808], P(('row', 'col')), may hold values from -1 to 1023, as said below
- reaction: float32 [131072], P(('row', 'col')), may hold values from 0.05 to 0.5
- load: float32 [131072], P(('row', 'col')), may hold values from -8 to 8
- area_normal: float32 [3, 55808], P(None, ('row', 'col')), may hold values from -2 to 2
Outputs:
- solution: float32 [131072], P(('row', 'col'))
- demag_potential: float32 [55808], P(('row', 'col'))
Inputs may be any that keep to these rules, and one draw needn't show every extreme that they name: `tet_nodes`: own node n of a partition lies in its layer n // 256; layers run along the grain, partitions of a grain follow their col index. Each column lists the corners of one tetrahedron as indices into the partition's ghost-extended list (see the steps); each lattice cell of a grain is split into six tetrahedra around one of its main diagonals, the same on every partition that lists them; every tetrahedron of the grain that has an own node of the partition as a corner stands exactly once on that partition; -1 marks an empty column, all four entries then -1. Tetrahedra have volumes bounded away from zero. `bnd_nodes`: each own node on the surface of its grain stands in exactly one slot of its partition; other slots hold -1. The partitions at the two ends of a grain fill all 436 slots. `node_coords`: node positions of the grains' meshes.
All inputs are finite; a program needn't handle non-finite values.
Results may differ from a plain program's by a relative error of at most 0.0003.
Values sent between devices are 32-bit elements; how exact they have to be, the bound alone decides.
A program may use at most 128 MiB of HBM per device.

v0:
```python
import math
import jax
import jax.numpy as jnp
from jax import lax
from jax.sharding import PartitionSpec as P

QS = 16
ITERS = 3


def extended_2(x, sides, width):
    for axis, dim in sides:
        devices, length = (lax.axis_size(axis), x.shape[dim])
        up = [(i, (i + 1) % devices) for i in range(devices - 1)]
        down = [(j, i) for i, j in up]
        last = lax.slice_in_dim(x, length - width, length, axis=dim)
        leading = lax.slice_in_dim(x, 0, width, axis=dim)
        before = lax.ppermute(last, axis, up)
        after = lax.ppermute(leading, axis, down)
        x = jnp.concatenate([before, x, after], axis=dim)
    return x


def cross_product(left_vec, right_vec):
    return jnp.stack(
        [
            left_vec[1] * right_vec[2] - left_vec[2] * right_vec[1],
            left_vec[2] * right_vec[0] - left_vec[0] * right_vec[2],
            left_vec[0] * right_vec[1] - left_vec[1] * right_vec[0],
        ]
    )


def element_matrices(ext_coords, corners):
    present = corners[0] >= 0
    corner_ids = jnp.maximum(corners, 0)
    vertex_zero = ext_coords[:, corner_ids[0]]
    edge_one = ext_coords[:, corner_ids[1]] - vertex_zero
    edge_two = ext_coords[:, corner_ids[2]] - vertex_zero
    edge_three = ext_coords[:, corner_ids[3]] - vertex_zero
    normal_one = cross_product(edge_two, edge_three)
    normal_two = cross_product(edge_three, edge_one)
    normal_three = cross_product(edge_one, edge_two)
    normal_zero = -(normal_one + normal_two + normal_three)
    volume_six = jnp.sum(edge_one * normal_one, axis=0)
    safe_volume = jnp.abs(jnp.where(present, volume_six, 1.0))
    weights = jnp.where(present, 1.0 / (6.0 * safe_volume), 0.0)
    normals = jnp.stack([normal_zero, normal_one, normal_two, normal_three])
    stiffness = jnp.sum(normals[:, None] * normals[None, :], axis=2) * weights
    return (stiffness, corner_ids)


def assemble(values, corner_ids, ext_len, own_count):
    accumulated = (
        jnp.zeros((ext_len,), values.dtype).at[corner_ids.reshape(-1)].add(values.reshape(-1))
    )
    margin = (ext_len - own_count) // 2
    return accumulated[margin : margin + own_count]


def tile_sum(targets, sources):
    delta_x = targets[0][:, None] - sources[0][None, :]
    delta_y = targets[1][:, None] - sources[1][None, :]
    delta_z = targets[2][:, None] - sources[2][None, :]
    distance = delta_x * delta_x + delta_y * delta_y + delta_z * delta_z + 0.25
    numerator = (
        delta_x * sources[3][None, :]
        + delta_y * sources[4][None, :]
        + delta_z * sources[5][None, :]
    )
    inverse = lax.rsqrt(distance)
    return jnp.sum(numerator * inverse * inverse * inverse, axis=1) * (0.25 / math.pi)


def blocked_sum(targets, sources, width):
    columns = sources.shape[1]
    blocks = sources.reshape(6, columns // width, width).transpose(1, 0, 2)

    def scan_step(running, src_block):
        return (running + tile_sum(targets, src_block), None)

    running, unused = lax.scan(scan_step, jnp.zeros((targets.shape[1],), jnp.float32), blocks)
    return running


def local(node_coords, tet_nodes, bnd_nodes, reaction, load, area_normal):
    square = QS * QS
    own_count = load.shape[0]
    ext_len = own_count + 2 * square
    ext_coords = extended_2(node_coords, (("col", 1),), square)
    stiffness, corner_ids = element_matrices(ext_coords, tet_nodes)
    diag_terms = jnp.stack([stiffness[k, k] for k in range(4)])
    diagonal = reaction + assemble(diag_terms, corner_ids, ext_len, own_count)
    solution = jnp.zeros_like(load)
    residual = load
    precond = residual / diagonal
    direction = precond
    rz_now = lax.psum(jnp.sum(residual * precond), ("row", "col"))
    for iteration in range(ITERS):
        extended = extended_2(direction, (("col", 0),), square)
        products = jnp.sum(stiffness * extended[corner_ids][None], axis=1)
        image = reaction * direction + assemble(products, corner_ids, ext_len, own_count)
        curvature = lax.psum(jnp.sum(direction * image), ("row", "col"))
        step_size = rz_now / curvature
        solution = solution + step_size * direction
        residual = residual - step_size * image
        if iteration + 1 < ITERS:
            precond = residual / diagonal
            rz_next = lax.psum(jnp.sum(residual * precond), ("row", "col"))
            direction = precond + rz_next / rz_now * direction
            rz_now = rz_next
    slot_count = bnd_nodes.shape[0]
    live_mask = (bnd_nodes >= 0).astype(jnp.float32)
    slot_ids = jnp.maximum(bnd_nodes, 0)
    positions = node_coords[:, slot_ids] * live_mask[None, :]
    traces = solution[slot_ids] * live_mask
    weighted = area_normal * traces[None, :]
    sources = jnp.concatenate([positions, weighted], axis=0)
    row_sums = blocked_sum(
        positions, lax.all_gather(sources, ("row", "col"), axis=1, tiled=True), 8 * slot_count
    )
    demag_potential = live_mask * (-0.5 * traces + row_sums)
    return (solution, demag_potential)


def solution(mesh):
    placed = (
        P(None, ("row", "col")),
        P(None, ("row", "col")),
        P(("row", "col")),
        P(("row", "col")),
        P(("row", "col")),
        P(None, ("row", "col")),
    )
    return jax.shard_map(
        local,
        mesh=mesh,
        in_specs=placed,
        out_specs=(P(("row", "col")), P(("row", "col"))),
        check_vma=False,
    )
```

profile of v0, /device:TPU:1, one launch (start us, length us, event | category | flops | bytes accessed | tf_op | source)
XLA Modules:
  0.0 1903.4 jit_solution(17606528600907032549)
XLA Ops:
  18.4 13.5 gather_fusion.1
  31.9 13.5 gather_fusion
  45.4 13.4 gather_fusion.2
  58.9 13.5 gather_fusion.3
  77.0 6.0 multiply_subtract_fusion.8
  83.0 10.5 multiply_reduce_fusion
  93.5 11.1 multiply_subtract_fusion.5
  104.7 6.6 multiply_subtract_fusion.2
  115.0 7.2 maximum_bitcast_fusion.1
  123.2 9.2 fusion.14
  132.4 10.1 pad_maximum_fusion
  142.5 7.9 copy.129
  150.5 8.0 copy.130
  159.3 150.8 %scatter_custom_fusion = f32[1536]{0:T(1024)S(1)} fusion(s32[27000]{0:T(1024)S(1)} %fusion.15, f32[27000]{0:T(1024)S(1)} %reshape.409, f32[]{:T(128)} %constant.18.clone.1), kind=kCustom, calls=%fused_computation.122 | custom fusion | flops 27000 | bytes 6148 | tf_op jit(solution)/shard_map/scatter-add | solution.py:55
  318.8 138.7 %gather_fusion.4 = f32[27000]{0:T(1024)S(1)} fusion(f32[1536]{0:T(1024)S(1)} %pad_maximum_fusion.4, s32[27648]{0:T(1024)S(1)} %pad_clamp_fusion), kind=kCustom, calls=%fused_computation.4 | custom fusion | bytes 324000 | tf_op jit(solution)/shard_map/gather | solution.py:101
  458.2 150.8 %scatter_custom_fusion.1 = f32[1536]{0:T(1024)S(1)} fusion(s32[27000]{0:T(1024)S(1)} %fusion.15, f32[27000]{0:T(1024)S(1)} %reshape.417, f32[]{:T(128)} %constant.18.clone.1), kind=kCustom, calls=%fused_computation.120 | custom fusion | flops 27000 | bytes 6148 | tf_op jit(solution)/shard_map/scatter-add | solution.py:55
  609.6 104.3 %all-reduce = (f32[]{:T(128)}, f32[]{:T(128)}) all-reduce(f32[]{:T(128)} %get-tuple-element.75, f32[]{:T(128)} %get-tuple-element.74), channel_id=1, replica_groups=mesh['row'=8,'col'=16] {'row','col'}, use_global_device_ids=true, to_apply=%region_4.5 | all-reduce | flops 2 | bytes 16 | tf_op jit(solution)/shard_map/psum | solution.py:98
  715.8 62.6 %psum.44 = f32[]{:T(128)} all-reduce(f32[]{:T(128)} %get-tuple-element.88), channel_id=1, replica_groups=mesh['row'=8,'col'=16] {'row','col'}, use_global_device_ids=true, to_apply=%region_10.11 | all-reduce | flops 1 | bytes 8 | tf_op jit(solution)/shard_map/psum | solution.py:109
  788.3 138.6 %gather_fusion.5 = f32[27000]{0:T(1024)S(1)} fusion(f32[1536]{0:T(1024)S(1)} %pad_maximum_fusion.5, s32[27648]{0:T(1024)S(1)} %pad_clamp_fusion), kind=kCustom, calls=%fused_computation.5 | custom fusion | bytes 324000 | tf_op jit(solution)/shard_map/gather | solution.py:101
  927.5 150.8 %scatter_custom_fusion.2 = f32[1536]{0:T(1024)S(1)} fusion(s32[27000]{0:T(1024)S(1)} %fusion.15, f32[27000]{0:T(1024)S(1)} %reshape.425, f32[]{:T(128)} %constant.18.clone.1), kind=kCustom, calls=%fused_computation.118 | custom fusion | flops 27000 | bytes 6148 | tf_op jit(solution)/shard_map/scatter-add | solution.py:55
  1078.8 80.1 %psum.45 = f32[]{:T(128)} all-reduce(f32[]{:T(128)} %multiply_reduce_fusion.6), channel_id=1, replica_groups=mesh['row'=8,'col'=16] {'row','col'}, use_global_device_ids=true, to_apply=%region_14.15 | all-reduce | flops 1 | bytes 8 | tf_op jit(solution)/shard_map/psum | solution.py:103
  1160.9 63.5 %psum.46 = f32[]{:T(128)} all-reduce(f32[]{:T(128)} %multiply_reduce_fusion.5), channel_id=1, replica_groups=mesh['row'=8,'col'=16] {'row','col'}, use_global_device_ids=true, to_apply=%region_16.17 | all-reduce | flops 1 | bytes 8 | tf_op jit(solution)/shard_map/psum | solution.py:109
  1233.0 138.6 %gather_fusion.6 = f32[27000]{0:T(1024)S(1)} fusion(f32[1536]{0:T(1024)S(1)} %pad_maximum_fusion.6, s32[27648]{0:T(1024)S(1)} %pad_clamp_fusion), kind=kCustom, calls=%fused_computation.6 | custom fusion | bytes 324000 | tf_op jit(solution)/shard_map/gather | solution.py:101
  1372.1 150.8 %scatter_custom_fusion.3 = f32[1536]{0:T(1024)S(1)} fusion(s32[27000]{0:T(1024)S(1)} %fusion.15, f32[27000]{0:T(1024)S(1)} %reshape.433, f32[]{:T(128)} %constant.18.clone.1), kind=kCustom, calls=%fused_computation.116 | custom fusion | flops 27000 | bytes 6148 | tf_op jit(solution)/shard_map/scatter-add | solution.py:55
  1524.9 81.0 %psum.47 = f32[]{:T(128)} all-reduce(f32[]{:T(128)} %fusion.21), channel_id=1, replica_groups=mesh['row'=8,'col'=16] {'row','col'}, use_global_device_ids=true, to_apply=%region_20.21 | all-reduce | flops 1 | bytes 8 | tf_op jit(solution)/shard_map/psum | solution.py:103
  1610.3 191.4 %all-gather.3.cloned.1.call-done = f32[128,436,6]{1,2,0:T(8,128)} async-done(((f32[1,436,6]{1,2,0:T(8,128)}), f32[128,436,6]{1,2,0:T(8,128)}) %all-gather.3.cloned.1.call-update) | async-done | bytes 1339408 | tf_op jit(solution)/shard_map/all_gather | solution.py:120
  1806.3 89.4 %while.11 = (s32[]{:T(128)}, f32[436]{0:T(512)S(1)}, f32[3,436]{1,0:T(4,128)S(1)}, f32[16,6,3488]{2,0,1:T(8,128)S(1)}, s32[]{:T(128)}, /*index=5*/s32[]{:T(128)}, s32[]{}, s32[]{}, s32[]{}, s32[]{}, /*index=10*/s32[]{}) while((s32[]{:T(128)}, f32[436]{0:T(512)S(1)}, f32[3,436]{1,0:T(4,128)S(1)}, f32[16,6,3488]{2,0,1:T(8,128)S(1)}, ...), condition=%wide.region_23.24_spmd.clone, body=%wide.region_21.23_spmd.clone.sunk | while | flops 27374704 | bytes 274011 | solution.py:82
  1806.6 5.3 fusion.44
  1812.2 5.3 fusion.44
  1817.8 5.3 fusion.44
  1823.4 5.3 fusion.44
  1829.0 5.3 fusion.44
  (165 shorter events, 122.3 us)
Async XLA Ops:
  7.2 1794.5 %all-gather.3.cloned.1.call-start = ((), (), s32[]{:S(2)}) async-start(), calls=%async_computation | async-start | bytes 2113536 | tf_op jit(solution)/shard_map/all_gather | solution.py:120
  7.9 9.4 collective-permute-start
  12.4 4.9 collective-permute-start.1
  77.0 6.1 copy-start.1
  93.5 11.1 copy-start.2
  104.7 6.6 copy-start.6
  111.3 3.6 copy-start.8
  115.0 7.2 copy-start.3
  115.0 7.2 copy-start.4
  115.0 7.2 copy-start.5
  115.0 8.3 copy-start.7
  150.5 159.6 %copy-start.9 = (f32[1024]{0:T(1024)S(1)}, f32[1024]{0:T(1024)}, u32[]{:S(2)}) copy-start(f32[1024]{0:T(1024)} %param.11) | copy-start | bytes 12292
  150.5 159.6 %copy-start.11 = (f32[1024]{0:T(1024)S(1)}, f32[1024]{0:T(1024)}, u32[]{:S(2)}) copy-start(f32[1024]{0:T(1024)} %param.12) | copy-start | bytes 12292
  310.1 5.8 collective-permute-start.2
  313.9 4.9 collective-permute-start.3
  779.8 5.5 collective-permute-start.4
  783.4 4.9 collective-permute-start.5
  788.3 372.6 %copy-start.13 = (s32[436]{0:T(512)S(1)}, s32[436]{0:T(512)}, u32[]{:S(2)}) copy-start(s32[436]{0:T(512)} %param.10) | copy-start | bytes 5236
  788.3 441.9 %copy-start.10 = (f32[3,1024]{1,0:T(4,128)S(1)}, f32[3,1024]{1,0:T(4,128)}, u32[]{:S(2)}) copy-start(f32[3,1024]{1,0:T(4,128)} %param.8) | copy-start | bytes 36868
  1225.8 4.6 collective-permute-start.6
  1228.1 4.9 collective-permute-start.7
  1371.5 238.1 %copy-start.12 = (f32[3,436]{1,0:T(4,128)S(1)}, f32[3,436]{1,0:T(4,128)}, u32[]{:S(2)}) copy-start(f32[3,436]{1,0:T(4,128)} %param.13) | copy-start | bytes 15700
  1607.2 198.2 %copy-start = (f32[1024]{0:T(1024)}, f32[1024]{0:T(1024)S(1)}, u32[]{:S(2)}) copy-start(f32[1024]{0:T(1024)S(1)} %multiply_add_fusion) | copy-start | bytes 12292
Sparse Core Ops, SparseCore 0:
  1610.4 191.2 all-gather.2
where the time goes:
time: 1910 us; the launch traced here: 1900 us
  other arithmetic  766 us (40%)
  local copies, waits for them, and re-layouts  502 us (26%)
  blocking collectives  392 us (21%)
  waiting for transfers between devices  200 us (10%)
  starting transfers between devices  22.1 us (1%)
  between operations  21.6 us (1%)
    scatter-add x4, other arithmetic, assemble(): jnp.zeros((ext_len,), values.dtype).at[corner_ids.reshape(-1)]  603 us
    gather x6, local copies, waits for them, and re-layouts, local(): products = jnp.sum(stiffness * extended[corner_ids][None], axis=1)  416 us
    all_gather x1, waiting for transfers between devices, local(): lax.all_gather(sources, ('row', 'col'), axis=1, tiled=True)  191 us
    psum x2, blocking collectives, local(): curvature = lax.psum(jnp.sum(direction * image), ('row', 'col'))  161 us
    psum x2, blocking collectives, local(): rz_next = lax.psum(jnp.sum(residual * precond), ('row', 'col'))  126 us
    psum x1, blocking collectives, local(): rz_now = lax.psum(jnp.sum(residual * precond), ('row', 'col'))  104 us
    reduce_sum x16, other arithmetic, tile_sum(): jnp.sum(numerator * inverse * inverse * inverse, axis=1) * (0.25 / math.pi)  84.6 us
  transfers between devices with their start and end apart: 9, of which 4 were waited for; matrix products, arithmetic and copies ran while one was open for 0% of the time, Pallas kernels for 0%

commit v1 on v0

--- a/solution.py
+++ b/solution.py
@@ -117,7 +117,14 @@
     weighted = area_normal * traces[None, :]
     sources = jnp.concatenate([positions, weighted], axis=0)
     row_sums = blocked_sum(
-        positions, lax.all_gather(sources, ("row", "col"), axis=1, tiled=True), 8 * slot_count
+        positions,
+        jnp.concatenate(
+            lax.all_to_all(
+                jnp.stack([sources] * lax.axis_size(("row", "col"))), ("row", "col"), 0, 0
+            ),
+            axis=1,
+        ),
+        8 * slot_count,
     )
     demag_potential = live_mask * (-0.5 * traces + row_sums)
     return (solution, demag_potential)

time: 1910 us -> 1750 us (0.916)
  waiting for transfers between devices: 200 us -> 39.2 us
    all_gather x1 -> x0, waiting for transfers between devices: 191 us -> none  [local(): lax.all_gather(sources, ('row', 'col'), axis=1, tiled=True)]
    all_to_all x0 -> x1, waiting for transfers between devices: none -> 30.7 us  [local(): lax.all_to_all(jnp.stack([sources] * lax.axis_size(('row', 'col'))), ('ro...]
where the time goes in v1:
time: 1750 us; the launch traced here: 1740 us
  other arithmetic  766 us (44%)
  local copies, waits for them, and re-layouts  503 us (29%)
  blocking collectives  392 us (22%)
  waiting for transfers between devices  39.2 us (2%)
  starting transfers between devices  27.6 us (2%)
    scatter-add x4, other arithmetic, assemble(): jnp.zeros((ext_len,), values.dtype).at[corner_ids.reshape(-1)]  603 us
    gather x6, local copies, waits for them, and re-layouts, local(): products = jnp.sum(stiffness * extended[corner_ids][None], axis=1)  416 us
    psum x2, blocking collectives, local(): curvature = lax.psum(jnp.sum(direction * image), ('row', 'col'))  161 us
    psum x2, blocking collectives, local(): rz_next = lax.psum(jnp.sum(residual * precond), ('row', 'col'))  126 us
    psum x1, blocking collectives, local(): rz_now = lax.psum(jnp.sum(residual * precond), ('row', 'col'))  104 us
    reduce_sum x16, other arithmetic, tile_sum(): jnp.sum(numerator * inverse * inverse * inverse, axis=1) * (0.25 / math.pi)  84.6 us
  transfers between devices with their start and end apart: 9, of which 4 were waited for; matrix products, arithmetic and copies ran while one was open for 0% of the time, Pallas kernels for 0%

profile of v1, /device:TPU:1, one launch (start us, length us, event | category | flops | bytes accessed | tf_op | source)
XLA Modules:
  0.0 1735.6 jit_solution(16594313370624064833)
XLA Ops:
  11.8 13.5 gather_fusion.1
  25.3 13.5 gather_fusion
  38.8 13.4 gather_fusion.2
  52.3 13.5 gather_fusion.3
  70.4 6.0 multiply_subtract_fusion.8
  76.4 10.5 multiply_reduce_fusion
  87.0 11.1 multiply_subtract_fusion.5
  98.1 6.6 multiply_subtract_fusion.2
  108.4 7.2 maximum_bitcast_fusion.1
  116.7 9.2 fusion.14
  125.9 10.1 pad_maximum_fusion
  135.9 7.9 copy.130
  143.9 8.0 copy.131
  152.7 150.8 %scatter_custom_fusion = f32[1536]{0:T(1024)S(1)} fusion(s32[27000]{0:T(1024)S(1)} %fusion.15, f32[27000]{0:T(1024)S(1)} %reshape.411, f32[]{:T(128)} %constant.18.clone.1), kind=kCustom, calls=%fused_computation.122 | custom fusion | flops 27000 | bytes 6148 | tf_op jit(solution)/shard_map/scatter-add | solution.py:55
  312.3 138.7 %gather_fusion.4 = f32[27000]{0:T(1024)S(1)} fusion(f32[1536]{0:T(1024)S(1)} %pad_maximum_fusion.5, s32[27648]{0:T(1024)S(1)} %pad_clamp_fusion), kind=kCustom, calls=%fused_computation.4 | custom fusion | bytes 324000 | tf_op jit(solution)/shard_map/gather | solution.py:101
  451.6 150.8 %scatter_custom_fusion.1 = f32[1536]{0:T(1024)S(1)} fusion(s32[27000]{0:T(1024)S(1)} %fusion.15, f32[27000]{0:T(1024)S(1)} %reshape.419, f32[]{:T(128)} %constant.18.clone.1), kind=kCustom, calls=%fused_computation.120 | custom fusion | flops 27000 | bytes 6148 | tf_op jit(solution)/shard_map/scatter-add | solution.py:55
  603.0 104.3 %all-reduce = (f32[]{:T(128)}, f32[]{:T(128)}) all-reduce(f32[]{:T(128)} %get-tuple-element.75, f32[]{:T(128)} %get-tuple-element.74), channel_id=1, replica_groups=mesh['row'=8,'col'=16] {'row','col'}, use_global_device_ids=true, to_apply=%region_4.5 | all-reduce | flops 2 | bytes 16 | tf_op jit(solution)/shard_map/psum | solution.py:98
  709.3 62.6 %psum.44 = f32[]{:T(128)} all-reduce(f32[]{:T(128)} %get-tuple-element.88), channel_id=1, replica_groups=mesh['row'=8,'col'=16] {'row','col'}, use_global_device_ids=true, to_apply=%region_10.11 | all-reduce | flops 1 | bytes 8 | tf_op jit(solution)/shard_map/psum | solution.py:109
  781.7 138.6 %gather_fusion.5 = f32[27000]{0:T(1024)S(1)} fusion(f32[1536]{0:T(1024)S(1)} %pad_maximum_fusion.6, s32[27648]{0:T(1024)S(1)} %pad_clamp_fusion), kind=kCustom, calls=%fused_computation.5 | custom fusion | bytes 324000 | tf_op jit(solution)/shard_map/gather | solution.py:101
  920.9 150.8 %scatter_custom_fusion.2 = f32[1536]{0:T(1024)S(1)} fusion(s32[27000]{0:T(1024)S(1)} %fusion.15, f32[27000]{0:T(1024)S(1)} %reshape.427, f32[]{:T(128)} %constant.18.clone.1), kind=kCustom, calls=%fused_computation.118 | custom fusion | flops 27000 | bytes 6148 | tf_op jit(solution)/shard_map/scatter-add | solution.py:55
  1072.3 80.1 %psum.45 = f32[]{:T(128)} all-reduce(f32[]{:T(128)} %multiply_reduce_fusion.6), channel_id=1, replica_groups=mesh['row'=8,'col'=16] {'row','col'}, use_global_device_ids=true, to_apply=%region_14.15 | all-reduce | flops 1 | bytes 8 | tf_op jit(solution)/shard_map/psum | solution.py:103
  1154.3 63.5 %psum.46 = f32[]{:T(128)} all-reduce(f32[]{:T(128)} %multiply_reduce_fusion.5), channel_id=1, replica_groups=mesh['row'=8,'col'=16] {'row','col'}, use_global_device_ids=true, to_apply=%region_16.17 | all-reduce | flops 1 | bytes 8 | tf_op jit(solution)/shard_map/psum | solution.py:109
  1226.4 138.6 %gather_fusion.6 = f32[27000]{0:T(1024)S(1)} fusion(f32[1536]{0:T(1024)S(1)} %pad_maximum_fusion.7, s32[27648]{0:T(1024)S(1)} %pad_clamp_fusion), kind=kCustom, calls=%fused_computation.6 | custom fusion | bytes 324000 | tf_op jit(solution)/shard_map/gather | solution.py:101
  1365.6 150.8 %scatter_custom_fusion.3 = f32[1536]{0:T(1024)S(1)} fusion(s32[27000]{0:T(1024)S(1)} %fusion.15, f32[27000]{0:T(1024)S(1)} %reshape.435, f32[]{:T(128)} %constant.18.clone.1), kind=kCustom, calls=%fused_computation.116 | custom fusion | flops 27000 | bytes 6148 | tf_op jit(solution)/shard_map/scatter-add | solution.py:55
  1518.3 81.0 %psum.47 = f32[]{:T(128)} all-reduce(f32[]{:T(128)} %fusion.21), channel_id=1, replica_groups=mesh['row'=8,'col'=16] {'row','col'}, use_global_device_ids=true, to_apply=%region_20.21 | all-reduce | flops 1 | bytes 8 | tf_op jit(solution)/shard_map/psum | solution.py:103
  1604.7 5.6 all-to-all-start
  1610.3 30.7 %all-to-all-done = f32[128,6,436]{2,1,0:T(8,128)S(1)} async-done(((f32[128,6,436]{2,1,0:T(8,128)}), f32[128,6,436]{2,1,0:T(8,128)S(1)}, u32[]{:S(2)}, u32[]{:S(2)}) %all-to-all-start) | async-done | bytes 1339424 | tf_op jit(solution)/shard_map/all_to_all | solution.py:122
  1645.4 89.4 %while.11 = (s32[]{:T(128)}, f32[436]{0:T(512)S(1)}, f32[3,436]{1,0:T(4,128)S(1)}, f32[16,6,3488]{2,0,1:T(8,128)S(1)}, s32[]{:T(128)}, /*index=5*/s32[]{:T(128)}, s32[]{}, s32[]{}, s32[]{}, s32[]{}, /*index=10*/s32[]{}) while((s32[]{:T(128)}, f32[436]{0:T(512)S(1)}, f32[3,436]{1,0:T(4,128)S(1)}, f32[16,6,3488]{2,0,1:T(8,128)S(1)}, ...), condition=%wide.region_23.24_spmd.clone, body=%wide.region_21.23_spmd.clone.sunk | while | flops 27374704 | bytes 274011 | solution.py:82
  1645.7 5.3 fusion.44
  1651.2 5.3 fusion.44
  1673.6 5.3 fusion.44
  1679.2 5.3 fusion.44
  (164 shorter events, 128.3 us)
Async XLA Ops:
  1.3 9.4 collective-permute-start
  5.8 4.9 collective-permute-start.1
  70.4 6.1 copy-start.1
  87.0 11.1 copy-start.2
  98.1 6.6 copy-start.6
  104.8 3.6 copy-start.8
  108.4 7.2 copy-start.3
  108.4 7.2 copy-start.4
  108.4 7.2 copy-start.5
  108.4 8.3 copy-start.7
  143.9 159.6 %copy-start.9 = (f32[1024]{0:T(1024)S(1)}, f32[1024]{0:T(1024)}, u32[]{:S(2)}) copy-start(f32[1024]{0:T(1024)} %param.11) | copy-start | bytes 12292
  143.9 159.6 %copy-start.11 = (f32[1024]{0:T(1024)S(1)}, f32[1024]{0:T(1024)}, u32[]{:S(2)}) copy-start(f32[1024]{0:T(1024)} %param.12) | copy-start | bytes 12292
  303.5 5.8 collective-permute-start.2
  307.4 4.9 collective-permute-start.3
  773.2 5.5 collective-permute-start.4
  776.8 4.9 collective-permute-start.5
  781.7 372.6 %copy-start.13 = (s32[436]{0:T(512)S(1)}, s32[436]{0:T(512)}, u32[]{:S(2)}) copy-start(s32[436]{0:T(512)} %param.10) | copy-start | bytes 5236
  781.7 441.9 %copy-start.10 = (f32[3,1024]{1,0:T(4,128)S(1)}, f32[3,1024]{1,0:T(4,128)}, u32[]{:S(2)}) copy-start(f32[3,1024]{1,0:T(4,128)} %param.8) | copy-start | bytes 36868
  1219.2 4.6 collective-permute-start.6
  1221.5 4.9 collective-permute-start.7
  1365.0 238.1 %copy-start.12 = (f32[3,436]{1,0:T(4,128)S(1)}, f32[3,436]{1,0:T(4,128)}, u32[]{:S(2)}) copy-start(f32[3,436]{1,0:T(4,128)} %param.13) | copy-start | bytes 15700
  1600.7 4.0 copy-start
  1604.7 36.3 %all-to-all-start = ((f32[128,6,436]{2,1,0:T(8,128)}), f32[128,6,436]{2,1,0:T(8,128)S(1)}, u32[]{:S(2)}, u32[]{:S(2)}) async-start(f32[128,6,436]{2,1,0:T(8,128)} %stack.62), calls=%async_computation | async-start | bytes 4194304 | tf_op jit(solution)/shard_map/all_to_all | solution.py:122
